TPU v7x, 32 devices: a whole 2x2x4 slice. The times are simulated.
32 devices in a mesh: dp: 8 (over z, x), tensor: 4 (over y, core).
Axes of the slice: x: 2, y: 2, z: 4, core: 2. Of those that a mesh axis runs over, the one named last changes fastest.
Arguments:
- hidden_in: bfloat16 [16384, 768], P('dp'), may hold values from -6 to 6
- doc_ids: int32 [16384], P('dp'), may hold values from 0 to 7, as said below
- ln1_gain: float32 [768], replicated, may hold values from 0.5 to 1.5
- ln1_bias: float32 [768], replicated, may hold values from -1.25 to 1.25
- w_qkv: bfloat16 [768, 3, 12, 64], P(None, None, 'tensor'), may hold values from -0.3125 to 0.3125
- b_qv: float32 [2, 12, 64], P(None, 'tensor'), may hold values from -1.75 to 1.75
- w_out: bfloat16 [12, 64, 768], P('tensor'), may hold values from -0.875 to 0.875
- b_out: float32 [768], replicated, may hold values from -1.25 to 1.25
- ln2_gain: float32 [768], replicated, may hold values from 0.5 to 1.5
- ln2_bias: float32 [768], replicated, may hold values from -1.25 to 1.25
- w_fc: bfloat16 [768, 3072], P(None, 'tensor'), may hold values from -0.21875 to 0.21875
- b_fc: float32 [24, 128], P('tensor'), may hold values from -1.75 to 1.75
- w_proj: bfloat16 [3072, 768], P('tensor'), may hold values from -0.109375 to 0.109375
- b_proj: float32 [768], replicated, may hold values from -1.25 to 1.25
- grad_out: bfloat16 [16384, 768], P('dp'), may hold values from -6 to 6
Outputs:
- block_out: bfloat16 [16384, 768], P('dp')
- grad_in: float32 [16384, 768], P('dp')
- grad_ln1_gain: float32 [768], P('dp')
- grad_ln1_bias: float32 [768], P('dp')
- grad_w_qkv: float32 [768, 3, 12, 64], P('dp', None, 'tensor')
- grad_b_qv: float32 [2, 12, 64], P(None, 'tensor', 'dp')
- grad_w_out: float32 [12, 64, 768], P('tensor', None, 'dp')
- grad_b_out: float32 [768], P('dp')
- grad_ln2_gain: float32 [768], P('dp')
- grad_ln2_bias: float32 [768], P('dp')
- grad_w_fc: float32 [768, 3072], P('dp', 'tensor')
- grad_b_fc: float32 [24, 128], P('tensor', 'dp')
- grad_w_proj: float32 [3072, 768], P('tensor', 'dp')
- grad_b_proj: float32 [768], P('dp')
Inputs may be any that keep to these rules, and one draw needn't show every extreme that they name: `doc_ids`: each aligned block of 2048 tokens (one index of dp) holds either 2048 // 1024 sequences of 1024 tokens or 8 sequences of 256 tokens, numbered from 0 in order; exactly half of the blocks hold the long ones.
All inputs are finite; a program needn't handle non-finite values.
Results may differ from a plain program's by a relative error of at most 0.015.
The roundings to bfloat16 on the way count: a program that leaves them out, or rounds other values in their place, can miss the bound.
Values may be sent and summed in bfloat16 or wider, within the bound.
No kernel may reach another device: no remote copies, remote signals or barrier semaphores. Data moves between devices by JAX's collectives and lax.ppermute only.
A program may use at most 192 MiB of HBM per device.

v0:
```python
import math
import jax
import jax.numpy as jnp
from jax import lax
from jax.sharding import PartitionSpec as P

EPSILON = 1e-05
MASKED = -1e30


def normalize(values):
    row_mean = jnp.mean(values, axis=-1, keepdims=True)
    centered = values - row_mean
    inv_std = lax.rsqrt(jnp.mean(centered * centered, axis=-1, keepdims=True) + EPSILON)
    return (centered * inv_std, inv_std)


def norm_back(grad_normed, normed, inv_std, gain_vec):
    scaled = grad_normed * gain_vec
    return inv_std * (
        scaled
        - jnp.mean(scaled, axis=-1, keepdims=True)
        - normed * jnp.mean(scaled * normed, axis=-1, keepdims=True)
    )


def masked_scores(queries, key_rows, row_ids, key_ids, start_row, scale_factor):
    scores = (
        jnp.einsum("qhd,khd->hqk", queries, key_rows, preferred_element_type=jnp.float32)
        * scale_factor
    )
    row_pos = start_row + jnp.arange(queries.shape[0])
    key_pos = jnp.arange(key_rows.shape[0])
    allowed = (row_pos[:, None] >= key_pos[None, :]) & (row_ids[:, None] == key_ids[None, :])
    return jnp.where(allowed[None], scores, MASKED)


def body(
    hidden_in,
    doc_ids,
    ln1_gain,
    ln1_bias,
    w_qkv,
    b_qv,
    w_out,
    b_out,
    ln2_gain,
    ln2_bias,
    w_fc,
    b_fc,
    w_proj,
    b_proj,
    grad_out,
):
    row_count, model_width = hidden_in.shape
    local_heads = w_qkv.shape[2]
    head_dim = w_qkv.shape[3]
    local_width = local_heads * head_dim
    hidden_units = w_fc.shape[1]
    scale_factor = 1.0 / math.sqrt(head_dim)
    block_rows = min(512, row_count)
    block_count = row_count // block_rows
    qkv_matrix = w_qkv.reshape(model_width, 3 * local_width)
    out_matrix = w_out.reshape(local_width, model_width)
    x_float = hidden_in.astype(jnp.float32)
    normed_one, inv_one = normalize(x_float)
    first_in = (normed_one * ln1_gain + ln1_bias).astype(jnp.bfloat16)
    projected = jnp.dot(first_in, qkv_matrix, preferred_element_type=jnp.float32).reshape(
        row_count, 3, local_heads, head_dim
    )
    queries = (projected[:, 0] + b_qv[0]).astype(jnp.bfloat16)
    key_rows = projected[:, 1].astype(jnp.bfloat16)
    value_rows = (projected[:, 2] + b_qv[1]).astype(jnp.bfloat16)
    attended_parts = []
    log_totals = []
    for block_index in range(block_count):
        start_row = block_index * block_rows
        end_row = start_row + block_rows
        scores = masked_scores(
            queries[start_row:end_row],
            key_rows[:end_row],
            doc_ids[start_row:end_row],
            doc_ids[:end_row],
            start_row,
            scale_factor,
        )
        row_max = jnp.max(scores, axis=-1, keepdims=True)
        exp_scores = jnp.exp(scores - row_max)
        row_total = jnp.sum(exp_scores, axis=-1, keepdims=True)
        weights_low = (exp_scores / row_total).astype(jnp.bfloat16)
        log_totals.append(row_max + jnp.log(row_total))
        attended_parts.append(
            jnp.einsum(
                "hqk,khd->qhd",
                weights_low,
                value_rows[:end_row],
                preferred_element_type=jnp.float32,
            )
        )
    attended = (
        jnp.concatenate(attended_parts, axis=0).reshape(row_count, local_width).astype(jnp.bfloat16)
    )
    branch_part = jnp.dot(attended, out_matrix, preferred_element_type=jnp.float32)
    branch = lax.psum(branch_part, "tensor") + b_out
    residual = x_float + branch
    normed_two, inv_two = normalize(residual)
    second_in = (normed_two * ln2_gain + ln2_bias).astype(jnp.bfloat16)
    pre_act = jnp.dot(second_in, w_fc, preferred_element_type=jnp.float32) + b_fc.reshape(
        hidden_units
    )
    act_value, gelu_back = jax.vjp(
        lambda pre_value: jax.nn.gelu(pre_value, approximate=True), pre_act
    )
    act_low = act_value.astype(jnp.bfloat16)
    mlp_part = jnp.dot(act_low, w_proj, preferred_element_type=jnp.float32)
    block_out = (
        residual + lax.psum(mlp_part.astype(jnp.bfloat16), "tensor").astype(jnp.float32) + b_proj
    )
    grad_float = grad_out.astype(jnp.float32)
    grad_w_proj = jnp.einsum("rf,rd->fd", act_low, grad_out, preferred_element_type=jnp.float32)
    grad_b_proj = jnp.sum(grad_float, axis=0)
    grad_act = jnp.einsum("rd,fd->rf", grad_out, w_proj, preferred_element_type=jnp.float32)
    grad_pre = gelu_back(grad_act)[0].astype(jnp.bfloat16)
    grad_w_fc = jnp.einsum("rd,rf->df", second_in, grad_pre, preferred_element_type=jnp.float32)
    grad_b_fc = jnp.sum(grad_pre.astype(jnp.float32), axis=0).reshape(b_fc.shape)
    grad_second_part = jnp.einsum("rf,df->rd", grad_pre, w_fc, preferred_element_type=jnp.float32)
    grad_second = lax.psum(grad_second_part, "tensor")
    grad_ln2_gain = jnp.sum(grad_second * normed_two, axis=0)
    grad_ln2_bias = jnp.sum(grad_second, axis=0)
    grad_residual = grad_float + norm_back(grad_second, normed_two, inv_two, ln2_gain)
    grad_branch = grad_residual.astype(jnp.bfloat16)
    grad_b_out = jnp.sum(grad_branch.astype(jnp.float32), axis=0)
    grad_w_out = jnp.einsum(
        "rc,rd->cd", attended, grad_branch, preferred_element_type=jnp.float32
    ).reshape(w_out.shape)
    grad_attended = (
        jnp.einsum("rd,cd->rc", grad_branch, out_matrix, preferred_element_type=jnp.float32)
        .astype(jnp.bfloat16)
        .reshape(row_count, local_heads, head_dim)
    )
    grad_query_parts = []
    grad_keys = jnp.zeros((row_count, local_heads, head_dim), jnp.float32)
    grad_values = jnp.zeros((row_count, local_heads, head_dim), jnp.float32)
    for block_index in range(block_count):
        start_row = block_index * block_rows
        end_row = start_row + block_rows
        block_queries = queries[start_row:end_row]
        scores = masked_scores(
            block_queries,
            key_rows[:end_row],
            doc_ids[start_row:end_row],
            doc_ids[:end_row],
            start_row,
            scale_factor,
        )
        attn_weights = jnp.exp(scores - log_totals[block_index])
        weights_low = attn_weights.astype(jnp.bfloat16)
        grad_rows = grad_attended[start_row:end_row]
        grad_weights = jnp.einsum(
            "qhd,khd->hqk", grad_rows, value_rows[:end_row], preferred_element_type=jnp.float32
        )
        row_delta = jnp.sum(attn_weights * grad_weights, axis=-1, keepdims=True)
        grad_scores = (attn_weights * (grad_weights - row_delta)).astype(jnp.bfloat16)
        grad_query_parts.append(
            jnp.einsum(
                "hqk,khd->qhd", grad_scores, key_rows[:end_row], preferred_element_type=jnp.float32
            )
            * scale_factor
        )
        grad_keys = grad_keys.at[:end_row].add(
            jnp.einsum(
                "hqk,qhd->khd", grad_scores, block_queries, preferred_element_type=jnp.float32
            )
            * scale_factor
        )
        grad_values = grad_values.at[:end_row].add(
            jnp.einsum("hqk,qhd->khd", weights_low, grad_rows, preferred_element_type=jnp.float32)
        )
    grad_queries = jnp.concatenate(grad_query_parts, axis=0)
    grad_mixed = jnp.stack([grad_queries, grad_keys, grad_values], axis=1).astype(jnp.bfloat16)
    grad_flat = grad_mixed.reshape(row_count, 3 * local_width)
    grad_w_qkv = jnp.einsum(
        "rd,rc->dc", first_in, grad_flat, preferred_element_type=jnp.float32
    ).reshape(w_qkv.shape)
    grad_b_qv = jnp.stack(
        [
            jnp.sum(grad_mixed[:, 0].astype(jnp.float32), axis=0),
            jnp.sum(grad_mixed[:, 2].astype(jnp.float32), axis=0),
        ],
        axis=0,
    )
    grad_first_part = jnp.einsum(
        "rc,dc->rd", grad_flat, qkv_matrix, preferred_element_type=jnp.float32
    )
    grad_first = lax.psum(grad_first_part.astype(jnp.bfloat16), "tensor").astype(jnp.float32)
    grad_ln1_gain = jnp.sum(grad_first * normed_one, axis=0)
    grad_ln1_bias = jnp.sum(grad_first, axis=0)
    grad_in = grad_residual + norm_back(grad_first, normed_one, inv_one, ln1_gain)
    shares = (
        lax.psum_scatter(grad_ln1_gain, "dp", scatter_dimension=0, tiled=True),
        lax.psum_scatter(grad_ln1_bias, "dp", scatter_dimension=0, tiled=True),
        lax.psum_scatter(grad_w_qkv, "dp", scatter_dimension=0, tiled=True),
        lax.psum_scatter(grad_b_qv, "dp", scatter_dimension=2, tiled=True),
        lax.psum_scatter(grad_w_out, "dp", scatter_dimension=2, tiled=True),
        lax.psum_scatter(grad_b_out, "dp", scatter_dimension=0, tiled=True),
        lax.psum_scatter(grad_ln2_gain, "dp", scatter_dimension=0, tiled=True),
        lax.psum_scatter(grad_ln2_bias, "dp", scatter_dimension=0, tiled=True),
        lax.psum_scatter(grad_w_fc, "dp", scatter_dimension=0, tiled=True),
        lax.psum_scatter(grad_b_fc, "dp", scatter_dimension=1, tiled=True),
        lax.psum_scatter(grad_w_proj, "dp", scatter_dimension=1, tiled=True),
        lax.psum_scatter(grad_b_proj, "dp", scatter_dimension=0, tiled=True),
    )
    return (
        block_out.astype(jnp.bfloat16),
        grad_in,
        shares[0],
        shares[1],
        shares[2],
        shares[3],
        shares[4],
        shares[5],
        shares[6],
        shares[7],
        shares[8],
        shares[9],
        shares[10],
        shares[11],
    )


def solution(mesh):
    in_specs = (
        P("dp", None),
        P("dp"),
        P(),
        P(),
        P(None, None, "tensor", None),
        P(None, "tensor", None),
        P("tensor", None, None),
        P(),
        P(),
        P(),
        P(None, "tensor"),
        P("tensor", None),
        P("tensor", None),
        P(),
        P("dp", None),
    )
    out_specs = (
        P("dp", None),
        P("dp", None),
        P("dp"),
        P("dp"),
        P("dp", None, "tensor", None),
        P(None, "tensor", "dp"),
        P("tensor", None, "dp"),
        P("dp"),
        P("dp"),
        P("dp"),
        P("dp", "tensor"),
        P("tensor", "dp"),
        P("tensor", "dp"),
        P("dp"),
    )
    return jax.shard_map(body, mesh=mesh, in_specs=in_specs, out_specs=out_specs, check_vma=False)
```

profile of v0, /device:TPU:0, one launch (start us, length us, event | category | flops | bytes accessed | tf_op | source)
XLA Modules:
  0.0 799.8 jit_solution(18134782078654954278)
XLA Ops:
  47.9 122.0 %all-reduce.15.cloned.1.call-done = f32[2048,768]{1,0:T(8,128)} async-done(((f32[2048,768]{1,0:T(8,128)}), f32[2048,768]{1,0:T(8,128)}) %all-reduce.15.cloned.1.call-update) | async-done | bytes 6291472 | tf_op jit(solution)/shard_map/psum | solution.py:104
  170.0 4.6 fusion.132
  180.7 7.7 convert_reduce_fusion.3
  190.0 4.5 fusion.142
  195.4 6.2 convolution_convert_fusion
  201.8 112.7 %all-reduce.17.cloned.1.call-done = f32[2048,768]{1,0:T(8,128)} async-done(((f32[2048,768]{1,0:T(8,128)}), f32[2048,768]{1,0:T(8,128)}) %all-reduce.17.cloned.1.call-update) | async-done | bytes 6291472 | tf_op jit(solution)/shard_map/psum | solution.py:127
  314.5 6.6 multiply_reduce_fusion.2
  321.8 5.8 convert_reduce_fusion.4
  341.1 5.7 multiply_reduce_fusion.1
  349.1 6.4 multiply_reduce_fusion
  369.2 5.4 multiply_convert_fusion.1
  377.1 6.3 multiply_convert_fusion
  393.6 5.5 bitcast_convert_fusion
  399.8 5.5 fusion.71
  408.2 6.9 fusion.143
  415.2 6.9 fusion.144
  425.8 29.0 %reduce-scatter.19.cloned.1.call-done = f32[96,192]{1,0:T(8,128)} async-done(((f32[768,192]{1,0:T(8,128)}), f32[96,192]{1,0:T(8,128)}) %reduce-scatter.19.cloned.1.call-update) | async-done | bytes 73744
  456.5 119.1 %all-reduce.19.cloned.1.call-done = (bf16[2048,768]{1,0:T(8,128)(2,1)}, bf16[2048,768]{1,0:T(8,128)(2,1)}) async-done(((bf16[2048,768]{1,0:T(8,128)(2,1)}, bf16[2048,768]{1,0:T(8,128)(2,1)}), (bf16[2048,768]{1,0:T(8,128)(2,1)}, bf16[2048,768]{1,0:T(8,128)(2,1)})) %all-reduce.19.cloned.1.call-update) | async-done | bytes 6291472 | tf_op jit(solution)/shard_map/psum | solution.py:117
  575.6 5.2 fusion.25
  580.9 38.1 %all-reduce.9 = (f32[768]{0:T(1024)S(1)}, f32[768]{0:T(1024)S(1)}, f32[2,3,64]{2,1,0:T(4,128)S(1)}, f32[768]{0:T(1024)S(1)}, f32[768]{0:T(1024)S(1)}, /*index=5*/f32[768]{0:T(1024)S(1)}, f32[768]{0:T(1024)S(1)}) all-reduce(f32[768]{0:T(1024)S(1)} %get-tuple-element.156, ...), channel_id=2, replica_groups=mesh['dp'=8,'tensor'=4] {'dp'}, use_global_device_ids=true, to_apply=%region_25.26.clone | all-reduce | flops 4992 | bytes 39936
  623.2 6.4 add_convert_fusion
  635.4 11.5 %reduce-scatter.17.cloned.1.call-done = f32[96,576]{1,0:T(8,128)} async-done(((f32[768,576]{1,0:T(8,128)}), f32[96,576]{1,0:T(8,128)}) %reduce-scatter.17.cloned.1.call-update) | async-done | bytes 221200
  648.8 70.8 %reduce-scatter.13.cloned.1.call-done = f32[96,768]{1,0:T(8,128)} async-done(((f32[768,768]{1,0:T(8,128)}), f32[96,768]{1,0:T(8,128)}) %reduce-scatter.13.cloned.1.call-update) | async-done | bytes 294928 | tf_op jit(solution)/shard_map/reduce_scatter | solution.py:208
  719.6 72.9 %reduce-scatter.15.cloned.1.call-done = f32[768,96]{0,1:T(8,128)} async-done(((f32[768,768]{0,1:T(8,128)}), f32[768,96]{0,1:T(8,128)}) %reduce-scatter.15.cloned.1.call-update) | async-done | bytes 294928 | tf_op jit(solution)/shard_map/reduce_scatter | solution.py:210
  (222 shorter events, 111.0 us)
Async XLA Ops:
  7.2 173.1 %copy-start = (bf16[768,768]{1,0:T(8,128)(2,1)S(1)}, bf16[768,768]{1,0:T(8,128)(2,1)}, u32[]{:S(2)}) copy-start(bf16[768,768]{1,0:T(8,128)(2,1)} %param.47) | copy-start | bytes 3538948
  7.2 8.2 %copy-start.33 = (f32[768]{0:T(1024)S(1)}, f32[768]{0:T(1024)}, u32[]{:S(2)}) copy-start(f32[768]{0:T(1024)} %param.37) | copy-start | bytes 9220
  7.2 8.2 %copy-start.39 = (bf16[768,3,3,64]{0,3,2,1:T(8,128)(2,1)S(1)}, bf16[768,3,3,64]{0,3,2,1:T(8,128)(2,1)}, u32[]{:S(2)}) copy-start(bf16[768,3,3,64]{0,3,2,1:T(8,128)(2,1)} %param.39) | copy-start | bytes 2654212
  7.2 8.2 %copy-start.41 = (f32[768]{0:T(1024)S(1)}, f32[768]{0:T(1024)}, u32[]{:S(2)}) copy-start(f32[768]{0:T(1024)} %param.38) | copy-start | bytes 9220
  7.2 162.7 %all-reduce.15.cloned.1.call-start = ((), (), s32[]{:S(2)}) async-start(), calls=%async_computation.5 | async-start | bytes 12582912 | tf_op jit(solution)/shard_map/psum | solution.py:104
  7.3 8.2 %copy-start.7 = (bf16[2048,768]{1,0:T(8,128)(2,1)S(1)}, bf16[2048,768]{1,0:T(8,128)(2,1)}, u32[]{:S(2)}) copy-start(bf16[2048,768]{1,0:T(8,128)(2,1)} %param.35) | copy-start | bytes 9437188
  18.0 14.2 %copy-start.13 = (bf16[2048,3,64]{0,2,1:T(8,128)(2,1)}, bf16[2048,3,64]{0,2,1:T(8,128)(2,1)S(1)}, u32[]{:S(2)}) copy-start(bf16[2048,3,64]{0,2,1:T(8,128)(2,1)S(1)} %get-tuple-element.180) | copy-start | bytes 2359300
  43.7 126.2 %copy-start.37 = (f32[768]{0:T(1024)S(1)}, f32[768]{0:T(1024)}, u32[]{:S(2)}) copy-start(f32[768]{0:T(1024)} %param.42) | copy-start | bytes 9220
  47.5 267.0 %all-reduce.17.cloned.1.call-start = ((), (), s32[]{:S(2)}) async-start(), calls=%async_computation.6 | async-start | bytes 12582912 | tf_op jit(solution)/shard_map/psum | solution.py:127
  194.5 229.6 %reduce-scatter.21.cloned.1.call-start = ((), (), s32[]{:S(2)}) async-start(), calls=%async_computation.11 | async-start | bytes 73728
  201.6 253.1 %reduce-scatter.19.cloned.1.call-start = ((), (), s32[]{:S(2)}) async-start(), calls=%async_computation.10 | async-start | bytes 884736
  341.1 7.8 slice-start.1
  391.1 184.6 %all-reduce.19.cloned.1.call-start = ((), (), s32[]{:S(2)}) async-start(), calls=%async_computation.12 | async-start | bytes 12582912 | tf_op jit(solution)/shard_map/psum | solution.py:117
  399.1 247.9 %reduce-scatter.17.cloned.1.call-start = ((), (), s32[]{:S(2)}) async-start(), calls=%async_computation.9 | async-start | bytes 2211840
  408.1 311.4 %reduce-scatter.13.cloned.1.call-start = ((), (), s32[]{:S(2)}) async-start(), calls=%async_computation.7 | async-start | bytes 2654208 | tf_op jit(solution)/shard_map/reduce_scatter | solution.py:208
  415.2 377.4 %reduce-scatter.15.cloned.1.call-start = ((), (), s32[]{:S(2)}) async-start(), calls=%async_computation.8 | async-start | bytes 2654208 | tf_op jit(solution)/shard_map/reduce_scatter | solution.py:210
  422.1 158.7 %copy-start.29 = (f32[768]{0:T(1024)S(1)}, f32[768]{0:T(1024)}, u32[]{:S(2)}) copy-start(f32[768]{0:T(1024)} %get-tuple-element.154) | copy-start | bytes 9220
  422.1 158.7 %copy-start.30 = (f32[768]{0:T(1024)S(1)}, f32[768]{0:T(1024)}, u32[]{:S(2)}) copy-start(f32[768]{0:T(1024)} %get-tuple-element.159) | copy-start | bytes 9220
  422.1 158.7 %copy-start.31 = (f32[768]{0:T(1024)S(1)}, f32[768]{0:T(1024)}, u32[]{:S(2)}) copy-start(f32[768]{0:T(1024)} %get-tuple-element.175) | copy-start | bytes 9220
  422.1 158.7 %copy-start.32 = (f32[768]{0:T(1024)S(1)}, f32[768]{0:T(1024)}, u32[]{:S(2)}) copy-start(f32[768]{0:T(1024)} %get-tuple-element.182) | copy-start | bytes 9220
  575.6 54.0 %slice-start.10 = ((s8[6291456]{0:T(1024)(128)(4,1)}), s8[2097152]{0:T(1024)(128)(4,1)S(1)}, s32[]{:S(2)}) async-start(s8[6291456]{0:T(1024)(128)(4,1)} %bitcast.204), calls=%async_computation.23 | async-start | bytes 4194304
  623.2 8.0 %copy-start.12 = (bf16[2048,768]{1,0:T(8,128)(2,1)S(1)}, bf16[2048,768]{1,0:T(8,128)(2,1)}, u32[]{:S(2)}) copy-start(bf16[2048,768]{1,0:T(8,128)(2,1)} %get-tuple-element.172) | copy-start | bytes 9437188
  623.2 8.0 %copy-start.35 = (f32[768]{0:T(1024)S(1)}, f32[768]{0:T(1024)}, u32[]{:S(2)}) copy-start(f32[768]{0:T(1024)} %param.37) | copy-start | bytes 9220
  623.2 169.3 %copy-start.1 = (bf16[768,768]{1,0:T(8,128)(2,1)S(1)}, bf16[768,768]{1,0:T(8,128)(2,1)}, u32[]{:S(2)}) copy-start(bf16[768,768]{1,0:T(8,128)(2,1)} %param.47) | copy-start | bytes 3538948
  (42 other events, 155.2 us)
Sparse Core Ops, SparseCore 0:
  47.6 122.2 all-reduce.14
  194.7 119.7 all-reduce.16
  318.5 62.7 reduce-scatter.20
  391.2 63.4 reduce-scatter.18
  457.0 118.6 all-reduce.18
  579.0 67.9 reduce-scatter.16
  651.0 68.4 reduce-scatter.12
  723.6 68.8 reduce-scatter.14
where the time goes:
time: 809 us; the launch traced here: 800 us
  waiting for transfers between devices  538 us (67%)
  matrix products  108 us (13%)
  other arithmetic  70 us (9%)
  blocking collectives  38.1 us (5%)
  local copies, waits for them, and re-layouts  27.9 us (3%)
  between operations  16.8 us (2%)
    psum x1, waiting for transfers between devices, body(): branch = lax.psum(branch_part, 'tensor') + b_out  122 us
    psum x1, waiting for transfers between devices, body(): lax.psum(mlp_part.astype(jnp.bfloat16), 'tensor').astype(jnp.float32)  119 us
    psum x1, waiting for transfers between devices, body(): grad_second = lax.psum(grad_second_part, 'tensor')  113 us
    reduce_scatter x1, waiting for transfers between devices, body(): lax.psum_scatter(grad_w_proj, 'dp', scatter_dimension=1, tiled=True)  72.9 us
    reduce_scatter x1, waiting for transfers between devices, body(): lax.psum_scatter(grad_w_fc, 'dp', scatter_dimension=0, tiled=True)  70.8 us
    unnamed x11, waiting for transfers between devices  40.6 us
    unnamed x1, blocking collectives  38.1 us
    unnamed x132, local copies, waits for them, and re-layouts  26.4 us
  transfers between devices with their start and end apart: 8, of which 7 were waited for; matrix products, arithmetic and copies ran while one was open for 17% of the time, Pallas kernels for 0%

commit v1 on v0

--- a/solution.py
+++ b/solution.py
@@ -114,7 +114,11 @@
     act_low = act_value.astype(jnp.bfloat16)
     mlp_part = jnp.dot(act_low, w_proj, preferred_element_type=jnp.float32)
     block_out = (
-        residual + lax.psum(mlp_part.astype(jnp.bfloat16), "tensor").astype(jnp.float32) + b_proj
+        residual
+        + jnp.sum(lax.all_gather(mlp_part.astype(jnp.bfloat16), "tensor"), axis=0).astype(
+            jnp.float32
+        )
+        + b_proj
     )
     grad_float = grad_out.astype(jnp.float32)
     grad_w_proj = jnp.einsum("rf,rd->fd", act_low, grad_out, preferred_element_type=jnp.float32)

time: 809 us -> 849 us (1.049)
  waiting for transfers between devices: 538 us -> 571 us
  other arithmetic: 70 us -> 80.3 us
    all_gather x0 -> x1, waiting for transfers between devices: none -> 78 us  [body(): lax.all_gather(mlp_part.astype(jnp.bfloat16), 'tensor')]
    psum x1, waiting for transfers between devices: 119 us -> 68 us  [body(): lax.psum(grad_first_part.astype(jnp.bfloat16), 'tensor').astype(jnp.float32)]
    reduce_sum x0 -> x1, other arithmetic: none -> 8.96 us  [body(): jnp.sum(lax.all_gather(mlp_part.astype(jnp.bfloat16), 'tensor'), axis=0)]
    unnamed x11 -> x12, waiting for transfers between devices: 40.6 us -> 46.7 us
    unnamed x132 -> x120, local copies, waits for them, and re-layouts: 26.4 us -> 23.8 us
  transfers between devices with their start and end apart: 8 -> 9, of which waited for: 7 -> 8; matrix products, arithmetic and copies ran while one was open for 17% -> 18% of each run, Pallas kernels for 0% -> 0%
where the time goes in v1:
time: 849 us; the launch traced here: 839 us
  waiting for transfers between devices  571 us (67%)
  matrix products  108 us (13%)
  other arithmetic  80.3 us (9%)
  blocking collectives  37.5 us (4%)
  local copies, waits for them, and re-layouts  25.3 us (3%)
  between operations  16.3 us (2%)
    psum x1, waiting for transfers between devices, body(): branch = lax.psum(branch_part, 'tensor') + b_out  122 us
    psum x1, waiting for transfers between devices, body(): grad_second = lax.psum(grad_second_part, 'tensor')  112 us
    all_gather x1, waiting for transfers between devices, body(): lax.all_gather(mlp_part.astype(jnp.bfloat16), 'tensor')  78 us
    reduce_scatter x1, waiting for transfers between devices, body(): lax.psum_scatter(grad_w_proj, 'dp', scatter_dimension=1, tiled=True)  72.9 us
    reduce_scatter x1, waiting for transfers between devices, body(): lax.psum_scatter(grad_w_fc, 'dp', scatter_dimension=0, tiled=True)  70.9 us
    psum x1, waiting for transfers between devices, body(): lax.psum(grad_first_part.astype(jnp.bfloat16), 'tensor').astype(jnp.float32)  68 us
    unnamed x12, waiting for transfers between devices  46.7 us
    unnamed x1, blocking collectives  37.5 us
  transfers between devices with their start and end apart: 9, of which 8 were waited for; matrix products, arithmetic and copies ran while one was open for 18% of the time, Pallas kernels for 0%

profile of v1, /device:TPU:0, one launch (start us, length us, event | category | flops | bytes accessed | tf_op | source)
XLA Modules:
  0.0 839.2 jit_solution(11356313275690501617)
XLA Ops:
  48.2 121.9 %all-reduce.14.cloned.1.call-done = f32[2048,768]{1,0:T(8,128)} async-done(((f32[2048,768]{1,0:T(8,128)}), f32[2048,768]{1,0:T(8,128)}) %all-reduce.14.cloned.1.call-update) | async-done | bytes 6291472 | tf_op jit(solution)/shard_map/psum | solution.py:104
  180.8 7.8 convert_reduce_fusion.3
  194.8 6.5 convolution_convert_fusion
  202.4 112.3 %all-reduce.16.cloned.1.call-done = f32[2048,768]{1,0:T(8,128)} async-done(((f32[2048,768]{1,0:T(8,128)}), f32[2048,768]{1,0:T(8,128)}) %all-reduce.16.cloned.1.call-update) | async-done | bytes 6291472 | tf_op jit(solution)/shard_map/psum | solution.py:131
  314.7 6.5 multiply_reduce_fusion.2
  321.2 78.0 %all-gather.3.cloned.1.call-done = bf16[8192,768]{1,0:T(8,128)(2,1)} async-done(((bf16[2048,768]{1,0:T(8,128)(2,1)}), bf16[8192,768]{1,0:T(8,128)(2,1)}) %all-gather.3.cloned.1.call-update) | async-done | bytes 12582928 | tf_op jit(solution)/shard_map/all_gather | solution.py:118
  399.1 9.0 %reduce_sum.245 = bf16[2048,768]{1,0:T(8,128)(2,1)} reduce(bf16[4,2048,768]{2,1,0:T(8,128)(2,1)} %bitcast.205, bf16[]{:T(256)} %constant.241.clone.1), dimensions={0}, to_apply=%region_13.14 | reduce | flops 4718592 | bytes 15728642 | tf_op jit(solution)/shard_map/reduce_sum | solution.py:118
  408.1 10.4 %convert_reduce_fusion.4 = (f32[768]{0:T(1024)}, f32[2048,768]{1,0:T(8,128)S(1)}, bf16[2048,768]{1,0:T(8,128)(2,1)}, f32[768]{0:T(1024)}) fusion(f32[2048]{0:T(1024)S(1)} %broadcast_multiply_fusion.2, f32[2048,768]{1,0:T(8,128)} %copy-done.3, f32[2048]{0:T(1024)S(1)} %broadcast_multiply_fusion.4, f32[2048]{0:T(1024)S(1)} %broadcast_multiply_fusion.3, ...), kind=kLoop, calls=%fused_computation.52 | loop fusion | flops 26737152 | bytes 28356608 | tf_op jit(solution)/shard_map/reduce_sum | solution.py:136
  432.0 5.7 multiply_reduce_fusion.1
  440.1 6.5 multiply_reduce_fusion
  460.0 5.4 multiply_convert_fusion.1
  468.0 6.3 multiply_convert_fusion
  484.9 5.2 bitcast_convert_fusion
  490.2 5.5 fusion.71
  498.6 6.9 fusion.143
  505.6 7.0 fusion.144
  516.3 29.5 %reduce-scatter.19.cloned.1.call-done = f32[96,192]{1,0:T(8,128)} async-done(((f32[768,192]{1,0:T(8,128)}), f32[96,192]{1,0:T(8,128)}) %reduce-scatter.19.cloned.1.call-update) | async-done | bytes 73744
  547.6 68.0 %all-reduce.18.cloned.1.call-done = bf16[2048,768]{1,0:T(8,128)(2,1)} async-done(((bf16[2048,768]{1,0:T(8,128)(2,1)}), bf16[2048,768]{1,0:T(8,128)(2,1)}) %all-reduce.18.cloned.1.call-update) | async-done | bytes 3145744 | tf_op jit(solution)/shard_map/psum | solution.py:199
  615.5 5.2 fusion.25
  620.8 37.5 %all-reduce.9 = (f32[768]{0:T(1024)S(1)}, f32[768]{0:T(1024)S(1)}, f32[2,3,64]{2,1,0:T(4,128)S(1)}, f32[768]{0:T(1024)S(1)}, f32[768]{0:T(1024)S(1)}, /*index=5*/f32[768]{0:T(1024)S(1)}, f32[768]{0:T(1024)S(1)}) all-reduce(f32[768]{0:T(1024)S(1)} %get-tuple-element.156, ...), channel_id=3, replica_groups=mesh['dp'=8,'tensor'=4] {'dp'}, use_global_device_ids=true, to_apply=%region_25.26.clone | all-reduce | flops 4992 | bytes 39936
  662.4 7.5 fusion.15
  670.0 17.0 %reduce-scatter.17.cloned.1.call-done = f32[96,576]{1,0:T(8,128)} async-done(((f32[768,576]{1,0:T(8,128)}), f32[96,576]{1,0:T(8,128)}) %reduce-scatter.17.cloned.1.call-update) | async-done | bytes 221200
  688.8 70.9 %reduce-scatter.13.cloned.1.call-done = f32[96,768]{1,0:T(8,128)} async-done(((f32[768,768]{1,0:T(8,128)}), f32[96,768]{1,0:T(8,128)}) %reduce-scatter.13.cloned.1.call-update) | async-done | bytes 294928 | tf_op jit(solution)/shard_map/reduce_scatter | solution.py:212
  759.6 72.9 %reduce-scatter.15.cloned.1.call-done = f32[768,96]{0,1:T(8,128)} async-done(((f32[768,768]{0,1:T(8,128)}), f32[768,96]{0,1:T(8,128)}) %reduce-scatter.15.cloned.1.call-update) | async-done | bytes 294928 | tf_op jit(solution)/shard_map/reduce_scatter | solution.py:214
  (212 shorter events, 113.7 us)
Async XLA Ops:
  7.2 173.2 %copy-start = (bf16[768,768]{1,0:T(8,128)(2,1)S(1)}, bf16[768,768]{1,0:T(8,128)(2,1)}, u32[]{:S(2)}) copy-start(bf16[768,768]{1,0:T(8,128)(2,1)} %param.47) | copy-start | bytes 3538948
  7.2 8.2 copy-start.27
  7.2 8.2 copy-start.35
  7.2 8.2 copy-start.37
  7.2 162.8 %all-reduce.14.cloned.1.call-start = ((), (), s32[]{:S(2)}) async-start(), calls=%async_computation.5 | async-start | bytes 12582912 | tf_op jit(solution)/shard_map/psum | solution.py:104
  7.3 8.2 copy-start.7
  18.0 14.3 %copy-start.10 = (bf16[2048,3,64]{0,2,1:T(8,128)(2,1)}, bf16[2048,3,64]{0,2,1:T(8,128)(2,1)S(1)}, u32[]{:S(2)}) copy-start(bf16[2048,3,64]{0,2,1:T(8,128)(2,1)S(1)} %get-tuple-element.179) | copy-start | bytes 2359300
  43.8 126.2 %copy-start.32 = (f32[768]{0:T(1024)S(1)}, f32[768]{0:T(1024)}, u32[]{:S(2)}) copy-start(f32[768]{0:T(1024)} %param.42) | copy-start | bytes 9220
  47.6 267.1 %all-reduce.16.cloned.1.call-start = ((), (), s32[]{:S(2)}) async-start(), calls=%async_computation.6 | async-start | bytes 12582912 | tf_op jit(solution)/shard_map/psum | solution.py:131
  194.7 204.4 %all-gather.3.cloned.1.call-start = ((), (), s32[]{:S(2)}) async-start(), calls=%async_computation.10 | async-start | bytes 15728640 | tf_op jit(solution)/shard_map/all_gather | solution.py:118
  201.3 313.3 %reduce-scatter.21.cloned.1.call-start = ((), (), s32[]{:S(2)}) async-start(), calls=%async_computation.13 | async-start | bytes 73728
  202.2 343.6 %reduce-scatter.19.cloned.1.call-start = ((), (), s32[]{:S(2)}) async-start(), calls=%async_computation.12 | async-start | bytes 884736
  399.1 9.0 %copy-start.33 = (f32[768]{0:T(1024)S(1)}, f32[768]{0:T(1024)}, u32[]{:S(2)}) copy-start(f32[768]{0:T(1024)} %param.48) | copy-start | bytes 9220
  432.0 7.8 slice-start
  432.0 7.8 slice-start.1
  482.4 133.2 %all-reduce.18.cloned.1.call-start = ((), (), s32[]{:S(2)}) async-start(), calls=%async_computation.7 | async-start | bytes 6291456 | tf_op jit(solution)/shard_map/psum | solution.py:199
  490.1 196.8 %reduce-scatter.17.cloned.1.call-start = ((), (), s32[]{:S(2)}) async-start(), calls=%async_computation.11 | async-start | bytes 2211840
  498.6 261.1 %reduce-scatter.13.cloned.1.call-start = ((), (), s32[]{:S(2)}) async-start(), calls=%async_computation.8 | async-start | bytes 2654208 | tf_op jit(solution)/shard_map/reduce_scatter | solution.py:212
  505.6 326.9 %reduce-scatter.15.cloned.1.call-start = ((), (), s32[]{:S(2)}) async-start(), calls=%async_computation.9 | async-start | bytes 2654208 | tf_op jit(solution)/shard_map/reduce_scatter | solution.py:214
  512.6 108.1 %copy-start.25 = (f32[768]{0:T(1024)S(1)}, f32[768]{0:T(1024)}, u32[]{:S(2)}) copy-start(f32[768]{0:T(1024)} %get-tuple-element.154) | copy-start | bytes 9220
  512.6 108.1 %copy-start.26 = (f32[768]{0:T(1024)S(1)}, f32[768]{0:T(1024)}, u32[]{:S(2)}) copy-start(f32[768]{0:T(1024)} %get-tuple-element.159) | copy-start | bytes 9220
  512.6 108.2 %copy-start.29 = (f32[768]{0:T(1024)S(1)}, f32[768]{0:T(1024)}, u32[]{:S(2)}) copy-start(f32[768]{0:T(1024)} %get-tuple-element.173) | copy-start | bytes 9220
  512.6 108.2 %copy-start.30 = (f32[768]{0:T(1024)S(1)}, f32[768]{0:T(1024)}, u32[]{:S(2)}) copy-start(f32[768]{0:T(1024)} %get-tuple-element.181) | copy-start | bytes 9220
  662.4 170.1 %copy-start.1 = (bf16[768,768]{1,0:T(8,128)(2,1)S(1)}, bf16[768,768]{1,0:T(8,128)(2,1)}, u32[]{:S(2)}) copy-start(bf16[768,768]{1,0:T(8,128)(2,1)} %param.47) | copy-start | bytes 3538948
  (37 other events, 139.4 us)
Sparse Core Ops, SparseCore 0:
  47.7 122.2 all-reduce.13
  194.9 119.7 all-reduce.15
  316.8 82.2 all-gather.2
  403.0 62.4 reduce-scatter.20
  482.5 63.2 reduce-scatter.18
  548.0 67.4 all-reduce.17
  619.0 67.8 reduce-scatter.16
  691.0 68.5 reduce-scatter.12
  763.7 68.7 reduce-scatter.14
